TPU v7x, 32 devices: a whole 2x2x4 slice. The times are simulated.
32 devices in a mesh: dp: 16 (over z, x, core), tensor: 2 (over y).
Axes of the slice: x: 2, y: 2, z: 4, core: 2. Of those that a mesh axis runs over, the one named last changes fastest.
Arguments:
- hidden_in: bfloat16 [4096, 1536], P(('dp', 'tensor')), may hold values from -6 to 6
- cotangent: float32 [4096, 1536], P(('dp', 'tensor')), may hold values from -6 to 6
- segments: int32 [16, 256], P('dp'), may hold values from 0 to 3, as said below
- positions: int32 [16, 256], P('dp'), may hold values from 0 to 127, as said below
- norm_gains: bfloat16 [1, 2, 1536], P(None, None, 'dp'), may hold values from 0.099609375 to 1.8984375
- q_weight: bfloat16 [1, 1536, 1536], P(None, 'dp', 'tensor'), may hold values from -0.15625 to 0.15625
- k_weight: bfloat16 [1, 1536, 256], P(None, 'dp', 'tensor'), may hold values from -0.15625 to 0.15625
- v_weight: bfloat16 [1, 1536, 256], P(None, 'dp', 'tensor'), may hold values from -0.15625 to 0.15625
- q_bias: bfloat16 [1, 12, 128], P(None, 'tensor', 'dp'), may hold values from -3 to 3
- k_bias: bfloat16 [1, 2, 128], P(None, 'tensor', 'dp'), may hold values from -3 to 3
- v_bias: bfloat16 [1, 2, 128], P(None, 'tensor', 'dp'), may hold values from -3 to 3
- o_weight: bfloat16 [1, 1536, 1536], P(None, 'tensor', 'dp'), may hold values from -0.625 to 0.625
- gate_weight: bfloat16 [1, 1536, 8960], P(None, 'dp', 'tensor'), may hold values from -0.15625 to 0.15625
- up_weight: bfloat16 [1, 1536, 8960], P(None, 'dp', 'tensor'), may hold values from -0.15625 to 0.15625
- down_weight: bfloat16 [1, 8960, 1536], P(None, 'tensor', 'dp'), may hold values from -0.0625 to 0.0625
Outputs:
- hidden_out: float32 [4096, 1536], P(('dp', 'tensor'))
- input_grad: float32 [4096, 1536], P(('dp', 'tensor'))
- gain_grads: float32 [1, 2, 1536], P(None, None, ('dp', 'tensor'))
- q_weight_grad: float32 [1, 1536, 1536], P(None, 'dp', 'tensor')
- k_weight_grad: float32 [1, 1536, 256], P(None, 'dp', 'tensor')
- v_weight_grad: float32 [1, 1536, 256], P(None, 'dp', 'tensor')
- o_weight_grad: float32 [1, 1536, 1536], P(None, 'tensor', 'dp')
- q_bias_grad: float32 [1, 12, 128], P(None, 'tensor', 'dp')
- k_bias_grad: float32 [1, 2, 128], P(None, 'tensor')
- v_bias_grad: float32 [1, 2, 128], P(None, 'tensor', 'dp')
- gate_weight_grad: float32 [1, 1536, 8960], P(None, 'dp', 'tensor')
- up_weight_grad: float32 [1, 1536, 8960], P(None, 'dp', 'tensor')
- down_weight_grad: float32 [1, 8960, 1536], P(None, 'tensor', 'dp')
Inputs may be any that keep to these rules, and one draw needn't show every extreme that they name: `segments`: document numbers never fall along a sequence and rise by one where a document starts; every sequence holds exactly 4 documents, one of them 256 / 2 tokens long. `positions`: A token's position within its document, 0 at the document's first token and rising by one.
All inputs are finite; a program needn't handle non-finite values.
Results may differ from a plain program's by a relative error of at most 0.02.
Values may be sent and summed in bfloat16 or wider, within the bound.
No kernel may reach another device: no remote copies, remote signals or barrier semaphores. Data moves between devices by JAX's collectives and lax.ppermute only.
A program may use at most 256 MiB of HBM per device.

v0:
```python
import jax
import jax.numpy as jnp
from jax import lax
from jax.sharding import PartitionSpec as P

HD = 128
LAYERS = 1
eps = 1e-06
theta_log = 13.815510557964274


def product(form, left, right):
    return jnp.einsum(form, left, right, preferred_element_type=jnp.float32)


def rope_tables(position_ids, head_width):
    half_width = head_width // 2
    freq_index = jnp.arange(half_width).astype(jnp.float32)
    frequency = jnp.exp(-(2.0 * freq_index / head_width) * theta_log)
    angles = position_ids.astype(jnp.float32)[..., None] * frequency
    return (jnp.cos(angles), jnp.sin(angles))


def rotate(vectors, cosine, sine_table):
    half_width = vectors.shape[-1] // 2
    first_half = vectors[..., :half_width]
    second_half = vectors[..., half_width:]
    cos_wide = cosine[:, :, None, :]
    sin_wide = sine_table[:, :, None, :]
    return jnp.concatenate(
        [
            first_half * cos_wide - second_half * sin_wide,
            second_half * cos_wide + first_half * sin_wide,
        ],
        axis=-1,
    )


def unrotate(vectors, cosine, sine_table):
    half_width = vectors.shape[-1] // 2
    first_half = vectors[..., :half_width]
    second_half = vectors[..., half_width:]
    cos_wide = cosine[:, :, None, :]
    sin_wide = sine_table[:, :, None, :]
    return jnp.concatenate(
        [
            first_half * cos_wide + second_half * sin_wide,
            second_half * cos_wide - first_half * sin_wide,
        ],
        axis=-1,
    )


def norm_forward(stream, gain_vec):
    inv_scale = lax.rsqrt(jnp.mean(stream * stream, axis=-1, keepdims=True) + eps)
    unit_rows = stream * inv_scale
    return ((unit_rows * gain_vec.astype(jnp.float32)).astype(jnp.bfloat16), unit_rows, inv_scale)


def norm_backward(d_normed, unit_rows, inv_scale, gain_vec):
    d_unit = d_normed * gain_vec.astype(jnp.float32)
    d_gain = jnp.sum(d_normed * unit_rows, axis=0)
    d_stream = inv_scale * (
        d_unit - unit_rows * jnp.mean(d_unit * unit_rows, axis=-1, keepdims=True)
    )
    return (d_stream, d_gain)


def attend(queries, key_vecs, value_vecs, allowed, scale):
    scores = product("bqngd,bknd->bngqk", queries, key_vecs) * scale
    expo = jnp.exp(scores) * allowed[:, None, None]
    denom_sum = jnp.sum(expo, axis=-1, keepdims=True)
    attention = (expo / denom_sum).astype(jnp.bfloat16)
    mixed = product("bngqk,bknd->bqngd", attention, value_vecs).astype(jnp.bfloat16)
    return (mixed, jnp.log(denom_sum))


def attend_backward(queries, key_vecs, value_vecs, allowed, log_total, d_mixed, scale):
    scores = product("bqngd,bknd->bngqk", queries, key_vecs) * scale
    probs_f = jnp.exp(scores - log_total) * allowed[:, None, None]
    d_value = product("bngqk,bqngd->bknd", probs_f.astype(jnp.bfloat16), d_mixed)
    d_probs = product("bqngd,bknd->bngqk", d_mixed, value_vecs)
    centre = jnp.sum(probs_f * d_probs, axis=-1, keepdims=True)
    d_scores = (probs_f * (d_probs - centre) * scale).astype(jnp.bfloat16)
    d_query = product("bngqk,bknd->bqngd", d_scores, key_vecs)
    d_key = product("bngqk,bqngd->bknd", d_scores, queries)
    return (d_query, d_key, d_value)


def attn_forward(rows_in, weights, cosine, sine_table, allowed, sequences):
    w_query, w_key, w_value, w_out, b_query, b_key, b_value = weights[:7]
    head_count, head_width = b_query.shape
    group_count = b_key.shape[0]
    group_size = head_count // group_count
    row_count = rows_in.shape[0]
    span_length = row_count // sequences
    queries = jnp.dot(rows_in, w_query, preferred_element_type=jnp.float32) + b_query.reshape(
        -1
    ).astype(jnp.float32)
    key_vecs = jnp.dot(rows_in, w_key, preferred_element_type=jnp.float32) + b_key.reshape(
        -1
    ).astype(jnp.float32)
    value_vecs = (
        jnp.dot(rows_in, w_value, preferred_element_type=jnp.float32)
        + b_value.reshape(-1).astype(jnp.float32)
    ).astype(jnp.bfloat16)
    queries = rotate(
        queries.reshape(sequences, span_length, head_count, head_width), cosine, sine_table
    ).astype(jnp.bfloat16)
    queries = queries.reshape(sequences, span_length, group_count, group_size, head_width)
    key_vecs = rotate(
        key_vecs.reshape(sequences, span_length, group_count, head_width), cosine, sine_table
    ).astype(jnp.bfloat16)
    value_vecs = value_vecs.reshape(sequences, span_length, group_count, head_width)
    mixed, log_total = attend(queries, key_vecs, value_vecs, allowed, head_width ** (-0.5))
    attn_rows = mixed.reshape(row_count, head_count * head_width)
    branch = jnp.dot(attn_rows, w_out, preferred_element_type=jnp.float32)
    return (branch, (queries, key_vecs, value_vecs, log_total, attn_rows))


def attn_backward(rows_in, weights, stored, d_out, cosine, sine_table, allowed, sequences):
    w_query, w_key, w_value, w_out, b_query, b_key, b_value = weights[:7]
    head_count, head_width = b_query.shape
    group_count = b_key.shape[0]
    queries, key_vecs, value_vecs, log_total, attn_rows = stored
    row_count = rows_in.shape[0]
    span_length = row_count // sequences
    d_o_weight = jnp.dot(attn_rows.T, d_out, preferred_element_type=jnp.float32)
    d_mixed = (
        jnp.dot(d_out, w_out.T, preferred_element_type=jnp.float32)
        .astype(jnp.bfloat16)
        .reshape(queries.shape)
    )
    d_query, d_key, d_value = attend_backward(
        queries, key_vecs, value_vecs, allowed, log_total, d_mixed, head_width ** (-0.5)
    )
    d_query = unrotate(
        d_query.reshape(sequences, span_length, head_count, head_width), cosine, sine_table
    ).reshape(row_count, -1)
    d_key = unrotate(d_key, cosine, sine_table).reshape(row_count, -1)
    d_value = d_value.reshape(row_count, -1)
    d_b_query = jnp.sum(d_query, axis=0).reshape(head_count, head_width)
    d_b_key = jnp.sum(d_key, axis=0).reshape(group_count, head_width)
    d_b_value = jnp.sum(d_value, axis=0).reshape(group_count, head_width)
    query_low = d_query.astype(jnp.bfloat16)
    key_low = d_key.astype(jnp.bfloat16)
    value_low = d_value.astype(jnp.bfloat16)
    d_rows = jnp.dot(query_low, w_query.T, preferred_element_type=jnp.float32)
    d_rows = d_rows + jnp.dot(key_low, w_key.T, preferred_element_type=jnp.float32)
    d_rows = d_rows + jnp.dot(value_low, w_value.T, preferred_element_type=jnp.float32)
    grads = (
        jnp.dot(rows_in.T, query_low, preferred_element_type=jnp.float32),
        jnp.dot(rows_in.T, key_low, preferred_element_type=jnp.float32),
        jnp.dot(rows_in.T, value_low, preferred_element_type=jnp.float32),
        d_o_weight,
        d_b_query,
        d_b_key,
        d_b_value,
    )
    return (d_rows, grads)


def mlp_forward(rows_in, weights):
    w_gate, w_up, w_down = weights[:3]
    gate_pre = jnp.dot(rows_in, w_gate, preferred_element_type=jnp.float32)
    up_pre = jnp.dot(rows_in, w_up, preferred_element_type=jnp.float32)
    hidden_act = (jax.nn.silu(gate_pre) * up_pre).astype(jnp.bfloat16)
    return (
        jnp.dot(hidden_act, w_down, preferred_element_type=jnp.float32),
        (gate_pre, up_pre, hidden_act),
    )


def mlp_backward(rows_in, weights, stored, d_out):
    w_gate, w_up, w_down = weights[:3]
    gate_pre, up_pre, hidden_act = stored
    d_down = jnp.dot(hidden_act.T, d_out, preferred_element_type=jnp.float32)
    d_hidden = jnp.dot(d_out, w_down.T, preferred_element_type=jnp.float32)
    sigmoid_g = jax.nn.sigmoid(gate_pre)
    d_gate = (d_hidden * up_pre * sigmoid_g * (1.0 + gate_pre * (1.0 - sigmoid_g))).astype(
        jnp.bfloat16
    )
    d_up = (d_hidden * gate_pre * sigmoid_g).astype(jnp.bfloat16)
    d_rows = jnp.dot(d_gate, w_gate.T, preferred_element_type=jnp.float32) + jnp.dot(
        d_up, w_up.T, preferred_element_type=jnp.float32
    )
    grads = (
        jnp.dot(rows_in.T, d_gate, preferred_element_type=jnp.float32),
        jnp.dot(rows_in.T, d_up, preferred_element_type=jnp.float32),
        d_down,
    )
    return (d_rows, grads)


def per_device(
    hidden_in,
    cotangent,
    segments,
    positions,
    norm_gains,
    q_weight,
    k_weight,
    v_weight,
    q_bias,
    k_bias,
    v_bias,
    o_weight,
    gate_weight,
    up_weight,
    down_weight,
):
    sequences = segments.shape[0]
    span_length = segments.shape[1]
    cosine, sine_table = rope_tables(positions, HD)
    places = jnp.arange(span_length)
    causal = places[None, :] <= places[:, None]
    allowed = ((segments[:, :, None] == segments[:, None, :]) & causal[None]).astype(jnp.float32)

    def fetch_attn(layer_no):
        return (
            lax.all_gather(q_weight[layer_no], "dp", axis=0, tiled=True),
            lax.all_gather(k_weight[layer_no], "dp", axis=0, tiled=True),
            lax.all_gather(v_weight[layer_no], "dp", axis=0, tiled=True),
            lax.all_gather(o_weight[layer_no], "dp", axis=1, tiled=True),
            lax.all_gather(q_bias[layer_no], "dp", axis=1, tiled=True),
            lax.all_gather(k_bias[layer_no], "dp", axis=1, tiled=True),
            lax.all_gather(v_bias[layer_no], "dp", axis=1, tiled=True),
            lax.all_gather(norm_gains[layer_no, 0], "dp", axis=0, tiled=True),
        )

    def fetch_mlp(layer_no):
        return (
            lax.all_gather(gate_weight[layer_no], "dp", axis=0, tiled=True),
            lax.all_gather(up_weight[layer_no], "dp", axis=0, tiled=True),
            lax.all_gather(down_weight[layer_no], "dp", axis=1, tiled=True),
            lax.all_gather(norm_gains[layer_no, 1], "dp", axis=0, tiled=True),
        )

    def gather_rows(values_in):
        return lax.all_gather(values_in, "tensor", axis=0, tiled=True)

    def sum_rows(partial_value):
        return lax.psum_scatter(
            partial_value.astype(jnp.bfloat16), "tensor", scatter_dimension=0, tiled=True
        ).astype(jnp.float32)

    stream = hidden_in.astype(jnp.float32)
    layer_no = 0
    attn_w = fetch_attn(layer_no)
    normed_one, unit_one, inv_one = norm_forward(stream, attn_w[7])
    rows_one = gather_rows(normed_one)
    partial_value, stored_one = attn_forward(
        rows_one, attn_w, cosine, sine_table, allowed, sequences
    )
    mid_stream = stream + sum_rows(partial_value)
    mlp_w = fetch_mlp(layer_no)
    normed_two, unit_two, inv_two = norm_forward(mid_stream, mlp_w[3])
    rows_two = gather_rows(normed_two)
    partial_value, stored_two = mlp_forward(rows_two, mlp_w)
    stream = mid_stream + sum_rows(partial_value)
    held = None
    kept = [
        (rows_one, unit_one, inv_one, stored_one, rows_two, unit_two, inv_two, stored_two, held)
    ]
    gradient = cotangent
    attn_list = []
    mlp_list = []
    gain_list = []
    key_list = []
    for layer_no in reversed(range(LAYERS)):
        rows_one, unit_one, inv_one, stored_one, rows_two, unit_two, inv_two, stored_two, held = (
            kept[layer_no]
        )
        mlp_w = fetch_mlp(layer_no)
        attn_w = fetch_attn(layer_no)
        d_rows, mlp_grads = mlp_backward(
            rows_two, mlp_w, stored_two, gather_rows(gradient.astype(jnp.bfloat16))
        )
        d_norm, gain_two = norm_backward(sum_rows(d_rows), unit_two, inv_two, mlp_w[3])
        grad_mid = gradient + d_norm
        mlp_list.insert(
            0,
            (
                lax.psum_scatter(mlp_grads[0], "dp", scatter_dimension=0, tiled=True),
                lax.psum_scatter(mlp_grads[1], "dp", scatter_dimension=0, tiled=True),
                lax.psum_scatter(mlp_grads[2], "dp", scatter_dimension=1, tiled=True),
            ),
        )
        d_rows, attn_grads = attn_backward(
            rows_one,
            attn_w,
            stored_one,
            gather_rows(grad_mid.astype(jnp.bfloat16)),
            cosine,
            sine_table,
            allowed,
            sequences,
        )
        d_norm, gain_one = norm_backward(sum_rows(d_rows), unit_one, inv_one, attn_w[7])
        gradient = grad_mid + d_norm
        spread_grads = (
            attn_grads[0],
            attn_grads[1],
            attn_grads[2],
            attn_grads[3],
            attn_grads[4],
            attn_grads[6],
        )
        attn_list.insert(
            0,
            (
                lax.psum_scatter(spread_grads[0], "dp", scatter_dimension=0, tiled=True),
                lax.psum_scatter(spread_grads[1], "dp", scatter_dimension=0, tiled=True),
                lax.psum_scatter(spread_grads[2], "dp", scatter_dimension=0, tiled=True),
                lax.psum_scatter(spread_grads[3], "dp", scatter_dimension=1, tiled=True),
                lax.psum_scatter(spread_grads[4], "dp", scatter_dimension=1, tiled=True),
                lax.psum_scatter(spread_grads[5], "dp", scatter_dimension=1, tiled=True),
            ),
        )
        key_list.insert(0, attn_grads[5])
        gain_list.insert(0, jnp.stack([gain_one, gain_two]))
    gain_grads = lax.psum_scatter(
        jnp.stack(gain_list), ("dp", "tensor"), scatter_dimension=2, tiled=True
    )
    key_bias_grad = lax.psum(jnp.stack(key_list), "dp")
    attn_out = tuple((jnp.stack([entry[index] for entry in attn_list]) for index in range(6)))
    mlp_out = tuple((jnp.stack([entry[index] for entry in mlp_list]) for index in range(3)))
    return (
        stream,
        gradient,
        gain_grads,
        attn_out[0],
        attn_out[1],
        attn_out[2],
        attn_out[3],
        attn_out[4],
        key_bias_grad,
        attn_out[5],
        mlp_out[0],
        mlp_out[1],
        mlp_out[2],
    )


def solution(mesh):
    return jax.shard_map(
        per_device,
        mesh=mesh,
        in_specs=(
            P(("dp", "tensor"), None),
            P(("dp", "tensor"), None),
            P("dp", None),
            P("dp", None),
            P(None, None, "dp"),
            P(None, "dp", "tensor"),
            P(None, "dp", "tensor"),
            P(None, "dp", "tensor"),
            P(None, "tensor", "dp"),
            P(None, "tensor", "dp"),
            P(None, "tensor", "dp"),
            P(None, "tensor", "dp"),
            P(None, "dp", "tensor"),
            P(None, "dp", "tensor"),
            P(None, "tensor", "dp"),
        ),
        out_specs=(
            P(("dp", "tensor"), None),
            P(("dp", "tensor"), None),
            P(None, None, ("dp", "tensor")),
            P(None, "dp", "tensor"),
            P(None, "dp", "tensor"),
            P(None, "dp", "tensor"),
            P(None, "tensor", "dp"),
            P(None, "tensor", "dp"),
            P(None, "tensor", None),
            P(None, "tensor", "dp"),
            P(None, "dp", "tensor"),
            P(None, "dp", "tensor"),
            P(None, "tensor", "dp"),
        ),
        check_vma=False,
    )
```

profile of v0, /device:TPU:0, one launch (start us, length us, event | category | flops | bytes accessed | tf_op | source)
XLA Modules:
  0.0 1799.2 jit_solution(1641613084074922660)
XLA Ops:
  15.7 37.0 %all-reduce.7 = (bf16[1536]{0:T(1024)(128)(2,1)S(1)}, bf16[128]{0:T(256)(128)(2,1)S(1)}, bf16[128]{0:T(256)(128)(2,1)S(1)}, bf16[1536]{0:T(1024)(128)(2,1)}) all-reduce(bf16[1536]{0:T(1024)(128)(2,1)S(1)} %dynamic-update-slice, bf16[128]{0:T(256)(128)(2,1)S(1)} %dynamic-update-slice.1, ...), channel_id=2, replica_groups=mesh['dp'=16,'tensor'=2] {'dp'}, use_global_device_ids=true, to_apply=%add | all-reduce | flops 3328 | bytes 13312
  52.7 17.3 all-gather.6
  71.2 21.7 %all-gather.1 = bf16[1,1536,128]{2,1,0:T(8,128)(2,1)S(1)} all-gather(bf16[1,96,128]{2,1,0:T(8,128)(2,1)} %param.22), channel_id=3, replica_groups=mesh['dp'=16,'tensor'=2] {'dp'}, dimensions={1}, use_global_device_ids=true | all-gather | bytes 417792 | tf_op jit(solution)/shard_map/all_gather | solution.py:223
  94.7 12.0 all_gather.58
  107.7 18.2 %all-gather.3 = bf16[1,1536,128]{2,1,0:T(8,128)(2,1)S(1)} all-gather(bf16[1,96,128]{2,1,0:T(8,128)(2,1)S(1)} %copy-done.33), channel_id=5, replica_groups=mesh['dp'=16,'tensor'=2] {'dp'}, dimensions={1}, use_global_device_ids=true | all-gather | bytes 417792 | tf_op jit(solution)/shard_map/all_gather | solution.py:222
  128.7 2.4 fusion.36
  135.2 3.5 convolution_convert_fusion
  142.4 20.3 %all_gather.71 = bf16[256,1536]{1,0:T(8,128)(2,1)} all-gather(bf16[128,1536]{1,0:T(8,128)(2,1)S(1)} %convert_element_type.173), channel_id=1, replica_groups=mesh['dp'=16,'tensor'=2] {'tensor'}, dimensions={0}, use_global_device_ids=true | all-gather | bytes 1179648 | tf_op jit(solution)/shard_map/all_gather | solution.py:240
  166.6 11.7 all_gather.67
  178.2 94.6 %all-gather.24.cloned.1.call-done = bf16[1,1536,4480]{2,1,0:T(8,128)(2,1)} async-done(((bf16[1,96,4480]{2,1,0:T(8,128)(2,1)}), bf16[1,1536,4480]{2,1,0:T(8,128)(2,1)}) %all-gather.24.cloned.1.call-update) | async-done | bytes 13762576 | tf_op jit(solution)/shard_map/all_gather | solution.py:234
  272.8 11.1 fusion.6
  283.9 96.9 %all-gather.26.cloned.1.call-done = bf16[1,4480,1536]{1,2,0:T(8,128)(2,1)} async-done(((bf16[1,4480,96]{1,2,0:T(8,128)(2,1)}), bf16[1,4480,1536]{1,2,0:T(8,128)(2,1)}) %all-gather.26.cloned.1.call-update) | async-done | bytes 13762576 | tf_op jit(solution)/shard_map/all_gather | solution.py:235
  380.9 11.0 fusion
  391.9 97.0 %all-gather.22.cloned.1.call-done = bf16[1,1536,4480]{2,1,0:T(8,128)(2,1)} async-done(((bf16[1,96,4480]{2,1,0:T(8,128)(2,1)}), bf16[1,1536,4480]{2,1,0:T(8,128)(2,1)}) %all-gather.22.cloned.1.call-update) | async-done | bytes 13762576 | tf_op jit(solution)/shard_map/all_gather | solution.py:233
  488.9 14.5 multiply_convert_fusion.1
  503.4 8.7 fusion.4
  512.1 8.3 fusion.18
  521.7 14.5 reduce-scatter.21.cloned.1.call-done
  536.2 2.1 fusion.59
  538.9 1.6 fusion.114
  540.5 11.3 all_gather.72
  552.7 1.5 fusion.40
  554.3 1.9 copy.80
  556.2 2.6 fusion.117
  564.9 2.5 fusion.25
  569.8 10.3 fusion.15
  581.5 5.9 reduce-scatter.23.cloned.1.call-done
  587.4 1.9 fusion.64
  590.6 2.4 copy.100
  593.3 2.2 fusion.98
  595.5 2.3 fusion.105
  597.9 2.9 fusion.118
  602.1 2.9 fusion.119
  606.1 12.8 fusion.120
  619.0 12.9 fusion.121
  633.1 13.0 fusion.122
  646.8 1.5 fusion.81
  649.2 34.1 %all-reduce.6 = (f32[6,128]{1,0:T(8,128)S(1)}, f32[1,1,128]{2,1,0:T(1,128)}, f32[1,128]{1,0:T(1,128)S(1)}) all-reduce(f32[6,128]{1,0:T(8,128)} %fusion.79, f32[1,1,128]{2,1,0:T(1,128)} %bitcast.241, f32[1,128]{1,0:T(1,128)} %bitcast.240), channel_id=23, replica_groups=mesh['dp'=16,'tensor'=2] {'dp'}, use_global_device_ids=true, to_apply=%region_18.19.clone | all-reduce | flops 1024 | bytes 8192
  685.2 2.8 fusion.55
  688.0 21.0 %reduce-scatter.39.cloned.1.call-done = f32[48,2]{1,0:T(8,128)} async-done(((f32[1536,2]{1,0:T(8,128)}), f32[48,2]{1,0:T(8,128)}) %reduce-scatter.39.cloned.1.call-update) | async-done | bytes 400
  709.0 1.4 copy.101
  710.4 58.7 %reduce-scatter.29.cloned.1.call-done = f32[96,128]{1,0:T(8,128)} async-done(((f32[1536,128]{1,0:T(8,128)}), f32[96,128]{1,0:T(8,128)}) %reduce-scatter.29.cloned.1.call-update) | async-done | bytes 49168 | tf_op jit(solution)/shard_map/reduce_scatter | solution.py:314
  769.1 59.8 %reduce-scatter.27.cloned.1.call-done = f32[96,128]{1,0:T(8,128)} async-done(((f32[1536,128]{1,0:T(8,128)}), f32[96,128]{1,0:T(8,128)}) %reduce-scatter.27.cloned.1.call-update) | async-done | bytes 49168 | tf_op jit(solution)/shard_map/reduce_scatter | solution.py:313
  828.9 79.1 %reduce-scatter.25.cloned.1.call-done = f32[96,768]{1,0:T(8,128)} async-done(((f32[1536,768]{1,0:T(8,128)}), f32[96,768]{1,0:T(8,128)}) %reduce-scatter.25.cloned.1.call-update) | async-done | bytes 294928 | tf_op jit(solution)/shard_map/reduce_scatter | solution.py:312
  908.0 79.1 %reduce-scatter.31.cloned.1.call-done = f32[768,96]{0,1:T(8,128)} async-done(((f32[768,1536]{0,1:T(8,128)}), f32[768,96]{0,1:T(8,128)}) %reduce-scatter.31.cloned.1.call-update) | async-done | bytes 294928 | tf_op jit(solution)/shard_map/reduce_scatter | solution.py:315
  987.1 268.5 %reduce-scatter.33.cloned.1.call-done = f32[96,4480]{1,0:T(8,128)} async-done(((f32[1536,4480]{1,0:T(8,128)}), f32[96,4480]{1,0:T(8,128)}) %reduce-scatter.33.cloned.1.call-update) | async-done | bytes 1720336 | tf_op jit(solution)/shard_map/reduce_scatter | solution.py:284
  1255.6 268.4 %reduce-scatter.35.cloned.1.call-done = f32[96,4480]{1,0:T(8,128)} async-done(((f32[1536,4480]{1,0:T(8,128)}), f32[96,4480]{1,0:T(8,128)}) %reduce-scatter.35.cloned.1.call-update) | async-done | bytes 1720336 | tf_op jit(solution)/shard_map/reduce_scatter | solution.py:285
  1524.0 268.4 %reduce-scatter.37.cloned.1.call-done = f32[4480,96]{0,1:T(8,128)} async-done(((f32[4480,1536]{0,1:T(8,128)}), f32[4480,96]{0,1:T(8,128)}) %reduce-scatter.37.cloned.1.call-update) | async-done | bytes 1720336 | tf_op jit(solution)/shard_map/reduce_scatter | solution.py:286
  (182 shorter events, 45.7 us)
Async XLA Ops:
  7.2 100.5 %copy-start.33 = (bf16[1,96,128]{2,1,0:T(8,128)(2,1)S(1)}, bf16[1,96,128]{2,1,0:T(8,128)(2,1)}, u32[]{:S(2)}) copy-start(bf16[1,96,128]{2,1,0:T(8,128)(2,1)} %param.21) | copy-start | bytes 73732
  7.2 121.5 %all-gather.18.cloned.1.call-start = ((), (), s32[]{:S(2)}) async-start(), calls=%async_computation.23 | async-start | bytes 2506752 | tf_op jit(solution)/shard_map/all_gather | solution.py:221
  7.9 127.3 %all-gather.20.cloned.1.call-start = ((), (), s32[]{:S(2)}) async-start(), calls=%async_computation.24 | async-start | bytes 2506752 | tf_op jit(solution)/shard_map/all_gather | solution.py:224
  8.7 154.9 %reduce-scatter.17.cloned.1.call-start = ((), (), s32[]{:S(2)}) async-start(), calls=%async_computation.12 | async-start | bytes 1179648 | tf_op jit(solution)/shard_map/reduce_scatter | solution.py:243
  12.0 115.3 %copy-start.34 = (f32[1,256]{1,0:T(1,128)}, f32[1,256]{1,0:T(1,128)S(1)}, u32[]{:S(2)}) copy-start(f32[1,256]{1,0:T(1,128)S(1)} %convert_element_type.156) | copy-start | bytes 3076
  70.0 57.3 %copy-start.37 = (f32[64]{0:T(128)}, f32[64]{0:T(128)S(1)}, u32[]{:S(2)}) copy-start(f32[64]{0:T(128)S(1)} %multiply_exponential_fusion) | copy-start | bytes 772
  92.9 13.8 copy-start.7
  94.7 33.8 %copy-start.40 = (s32[1,256]{1,0:T(1,128)S(1)}, s32[1,256]{1,0:T(1,128)}, u32[]{:S(2)}) copy-start(s32[1,256]{1,0:T(1,128)} %param.17) | copy-start | bytes 3076
  125.9 5.2 copy-start.5
  131.7 2.2 copy-start.25
  131.7 2.2 copy-start.27
  132.0 2.6 copy-start.29
  133.2 1.8 copy-start.9
  135.2 4.1 copy-start.20
  138.7 24.9 %copy-start = (bf16[128,1536]{1,0:T(8,128)(2,1)S(1)}, bf16[128,1536]{1,0:T(8,128)(2,1)}, u32[]{:S(2)}) copy-start(bf16[128,1536]{1,0:T(8,128)(2,1)} %param.15) | copy-start | bytes 1179652
  138.7 134.1 %all-gather.24.cloned.1.call-start = ((), (), s32[]{:S(2)}) async-start(), calls=%async_computation.26 | async-start | bytes 14622720 | tf_op jit(solution)/shard_map/all_gather | solution.py:234
  139.3 241.5 %all-gather.26.cloned.1.call-start = ((), (), s32[]{:S(2)}) async-start(), calls=%async_computation.27 | async-start | bytes 14622720 | tf_op jit(solution)/shard_map/all_gather | solution.py:235
  139.9 349.0 %all-gather.22.cloned.1.call-start = ((), (), s32[]{:S(2)}) async-start(), calls=%async_computation.25 | async-start | bytes 14622720 | tf_op jit(solution)/shard_map/all_gather | solution.py:233
  140.5 395.8 %reduce-scatter.21.cloned.1.call-start = ((), (), s32[]{:S(2)}) async-start(), calls=%async_computation.14 | async-start | bytes 1179648 | tf_op jit(solution)/shard_map/reduce_scatter | solution.py:243
  503.4 8.7 copy-start.17
  503.4 8.7 copy-start.18
  512.1 24.2 %copy-start.1 = (bf16[128,1536]{1,0:T(8,128)(2,1)S(1)}, bf16[128,1536]{1,0:T(8,128)(2,1)}, u32[]{:S(2)}) copy-start(bf16[128,1536]{1,0:T(8,128)(2,1)} %reduce-scatter.17.cloned.1.call-done) | copy-start | bytes 1179652
  520.4 67.0 %reduce-scatter.23.cloned.1.call-start = ((), (), s32[]{:S(2)}) async-start(), calls=%async_computation.15 | async-start | bytes 1179648 | tf_op jit(solution)/shard_map/reduce_scatter | solution.py:243
  536.2 16.5 copy-start.42
  556.2 2.7 copy-start.4
  556.2 2.7 copy-start.30
  556.2 2.7 copy-start.31
  559.3 1.7 copy-start.26
  559.3 1.7 copy-start.28
  560.4 2.0 copy-start.19
  564.9 2.6 copy-start.6
  564.9 2.6 copy-start.22
  564.9 2.6 copy-start.23
  569.8 115.4 %reduce-scatter.19.cloned.1.call-start = ((), (), s32[]{:S(2)}) async-start(), calls=%async_computation.13 | async-start | bytes 1179648 | tf_op jit(solution)/shard_map/reduce_scatter | solution.py:243
  580.2 128.9 %reduce-scatter.39.cloned.1.call-start = ((), (), s32[]{:S(2)}) async-start(), calls=%async_computation.28 | async-start | bytes 811008
  593.0 176.1 %reduce-scatter.29.cloned.1.call-start = ((), (), s32[]{:S(2)}) async-start(), calls=%async_computation.18 | async-start | bytes 835584 | tf_op jit(solution)/shard_map/reduce_scatter | solution.py:314
  595.5 233.4 %reduce-scatter.27.cloned.1.call-start = ((), (), s32[]{:S(2)}) async-start(), calls=%async_computation.17 | async-start | bytes 835584 | tf_op jit(solution)/shard_map/reduce_scatter | solution.py:313
  597.8 310.2 %reduce-scatter.25.cloned.1.call-start = ((), (), s32[]{:S(2)}) async-start(), calls=%async_computation.16 | async-start | bytes 5013504 | tf_op jit(solution)/shard_map/reduce_scatter | solution.py:312
  600.8 1.1 copy-start.15
  600.8 1.2 copy-start.21
  600.8 386.3 %reduce-scatter.31.cloned.1.call-start = ((), (), s32[]{:S(2)}) async-start(), calls=%async_computation.19 | async-start | bytes 5013504 | tf_op jit(solution)/shard_map/reduce_scatter | solution.py:315
  605.0 1.1 copy-start.3
  605.0 650.6 %reduce-scatter.33.cloned.1.call-start = ((), (), s32[]{:S(2)}) async-start(), calls=%async_computation.20 | async-start | bytes 29245440 | tf_op jit(solution)/shard_map/reduce_scatter | solution.py:284
  619.0 905.1 %reduce-scatter.35.cloned.1.call-start = ((), (), s32[]{:S(2)}) async-start(), calls=%async_computation.21 | async-start | bytes 29245440 | tf_op jit(solution)/shard_map/reduce_scatter | solution.py:285
  631.9 1.1 copy-start.16
  632.0 1160.5 %reduce-scatter.37.cloned.1.call-start = ((), (), s32[]{:S(2)}) async-start(), calls=%async_computation.22 | async-start | bytes 29245440 | tf_op jit(solution)/shard_map/reduce_scatter | solution.py:286
  646.0 39.2 %copy-start.13 = (bf16[128,1536]{1,0:T(8,128)(2,1)S(1)}, bf16[128,1536]{1,0:T(8,128)(2,1)}, u32[]{:S(2)}) copy-start(bf16[128,1536]{1,0:T(8,128)(2,1)} %reduce-scatter.21.cloned.1.call-done) | copy-start | bytes 1179652
  646.1 39.1 %copy-start.2 = (f32[128,1536]{1,0:T(8,128)S(1)}, f32[128,1536]{1,0:T(8,128)}, u32[]{:S(2)}) copy-start(f32[128,1536]{1,0:T(8,128)} %param.16) | copy-start | bytes 2359300
  (12 other events, 10.1 us)
Sparse Core Ops, SparseCore 0:
  10.3 45.3 all-gather.17
  57.9 41.1 all-gather.19
  138.8 24.7 reduce-scatter.16
  165.8 107.0 all-gather.23
  275.0 105.8 all-gather.25
  383.0 105.8 all-gather.21
  520.5 15.6 reduce-scatter.20
  569.9 17.5 reduce-scatter.22
  590.3 17.4 reduce-scatter.18
  612.8 96.2 reduce-scatter.38
  713.2 55.9 reduce-scatter.28
  773.1 55.7 reduce-scatter.26
  833.4 74.5 reduce-scatter.24
  912.3 74.8 reduce-scatter.30
  991.7 263.9 reduce-scatter.32
  1260.2 263.8 reduce-scatter.34
  1528.6 263.8 reduce-scatter.36
where the time goes:
time: 1810 us; the launch traced here: 1800 us
  waiting for transfers between devices  1420 us (78%)
  blocking collectives  184 us (10%)
  matrix products  131 us (7%)
  other arithmetic  26.2 us (1%)
  local copies, waits for them, and re-layouts  24.6 us (1%)
    reduce_scatter x1, waiting for transfers between devices, per_device(): lax.psum_scatter(mlp_grads[0], 'dp', scatter_dimension=0, tiled=True)  268 us
    reduce_scatter x1, waiting for transfers between devices, per_device(): lax.psum_scatter(mlp_grads[1], 'dp', scatter_dimension=0, tiled=True)  268 us
    reduce_scatter x1, waiting for transfers between devices, per_device(): lax.psum_scatter(mlp_grads[2], 'dp', scatter_dimension=1, tiled=True)  268 us
    all_gather x1, waiting for transfers between devices, fetch_mlp(): lax.all_gather(gate_weight[layer_no], 'dp', axis=0, tiled=True)  97 us
    all_gather x1, waiting for transfers between devices, fetch_mlp(): lax.all_gather(down_weight[layer_no], 'dp', axis=1, tiled=True)  96.9 us
    all_gather x1, waiting for transfers between devices, fetch_mlp(): lax.all_gather(up_weight[layer_no], 'dp', axis=0, tiled=True)  94.6 us
    reduce_scatter x1, waiting for transfers between devices, per_device(): lax.psum_scatter(spread_grads[3], 'dp', scatter_dimension=1, tiled=True)  79.1 us
    reduce_scatter x1, waiting for transfers between devices, per_device(): lax.psum_scatter(spread_grads[0], 'dp', scatter_dimension=0, tiled=True)  79.1 us
  transfers between devices with their start and end apart: 17, of which 14 were waited for; matrix products, arithmetic and copies ran while one was open for 7% of the time, Pallas kernels for 0%

commit v1 on v0

--- a/solution.py
+++ b/solution.py
@@ -2,11 +2,18 @@
 import jax.numpy as jnp
 from jax import lax
 from jax.sharding import PartitionSpec as P
+from jax.lax import axis_index, axis_size, ppermute
 
 HD = 128
 LAYERS = 1
 eps = 1e-06
 theta_log = 13.815510557964274
+
+
+def reach_the_core(patch, at_axis):
+    plain = list(patch.shape[1:])
+    plain[at_axis] *= patch.shape[0]
+    return jnp.moveaxis(patch, 0, at_axis).reshape(plain)
 
 
 def product(form, left, right):
@@ -229,9 +236,20 @@
         )
 
     def fetch_mlp(layer_no):
+
+        def see_the_stops_all(in_array, mesh_name, dim_no):
+            nd = axis_size(mesh_name)
+            grid = tuple(((to_i, (to_i + 1) % nd) for to_i in range(nd)))
+            sheets = [in_array]
+            while len(sheets) < nd:
+                sheets.append(ppermute(sheets[-1], mesh_name, grid))
+            v_next = axis_index(mesh_name)
+            sheets = jnp.stack(sheets)[(v_next - jnp.arange(nd)) % nd]
+            return reach_the_core(sheets, dim_no)
+
         return (
             lax.all_gather(gate_weight[layer_no], "dp", axis=0, tiled=True),
-            lax.all_gather(up_weight[layer_no], "dp", axis=0, tiled=True),
+            see_the_stops_all(up_weight[layer_no], "dp", dim_no=0),
             lax.all_gather(down_weight[layer_no], "dp", axis=1, tiled=True),
             lax.all_gather(norm_gains[layer_no, 1], "dp", axis=0, tiled=True),
         )

time: 1810 us -> 1850 us (1.022)
  local copies, waits for them, and re-layouts: 24.6 us -> 55 us
    ppermute x0 -> x15, waiting for transfers between devices: none -> 305 us  [see_the_stops_all(): sheets.append(ppermute(sheets[-1], mesh_name, grid))]
    all_gather x1, waiting for transfers between devices: 97 us -> 0.01 us  [fetch_mlp(): lax.all_gather(gate_weight[layer_no], 'dp', axis=0, tiled=True)]
    all_gather x1, waiting for transfers between devices: 96.9 us -> 0.01 us  [fetch_mlp(): lax.all_gather(down_weight[layer_no], 'dp', axis=1, tiled=True)]
    all_gather x1 -> x0, waiting for transfers between devices: 94.6 us -> none  [fetch_mlp(): lax.all_gather(up_weight[layer_no], 'dp', axis=0, tiled=True)]
  transfers between devices with their start and end apart: 17 -> 31, of which waited for: 14 -> 24; matrix products, arithmetic and copies ran while one was open for 7% -> 8% of each run, Pallas kernels for 0% -> 0%
where the time goes in v1:
time: 1850 us; the launch traced here: 1840 us
  waiting for transfers between devices  1430 us (77%)
  blocking collectives  180 us (10%)
  matrix products  128 us (7%)
  local copies, waits for them, and re-layouts  55 us (3%)
  other arithmetic  27.8 us (2%)
    ppermute x15, waiting for transfers between devices, see_the_stops_all(): sheets.append(ppermute(sheets[-1], mesh_name, grid))  305 us
    reduce_scatter x1, waiting for transfers between devices, per_device(): lax.psum_scatter(mlp_grads[0], 'dp', scatter_dimension=0, tiled=True)  269 us
    reduce_scatter x1, waiting for transfers between devices, per_device(): lax.psum_scatter(mlp_grads[2], 'dp', scatter_dimension=1, tiled=True)  268 us
    reduce_scatter x1, waiting for transfers between devices, per_device(): lax.psum_scatter(mlp_grads[1], 'dp', scatter_dimension=0, tiled=True)  268 us
    reduce_scatter x1, waiting for transfers between devices, per_device(): lax.psum_scatter(spread_grads[3], 'dp', scatter_dimension=1, tiled=True)  79.2 us
    reduce_scatter x1, waiting for transfers between devices, per_device(): lax.psum_scatter(spread_grads[0], 'dp', scatter_dimension=0, tiled=True)  78.9 us
    unnamed x2, blocking collectives  71.4 us
    reduce_scatter x1, waiting for transfers between devices, per_device(): lax.psum_scatter(spread_grads[2], 'dp', scatter_dimension=0, tiled=True)  59.9 us
  transfers between devices with their start and end apart: 31, of which 24 were waited for; matrix products, arithmetic and copies ran while one was open for 8% of the time, Pallas kernels for 0%

profile of v1, /device:TPU:0, one launch (start us, length us, event | category | flops | bytes accessed | tf_op | source)
XLA Modules:
  0.0 1839.3 jit_solution(1008463641297857062)
XLA Ops:
  14.3 37.1 %all-reduce.7 = (bf16[1536]{0:T(1024)(128)(2,1)S(1)}, bf16[128]{0:T(256)(128)(2,1)S(1)}, bf16[128]{0:T(256)(128)(2,1)S(1)}, bf16[1536]{0:T(1024)(128)(2,1)}) all-reduce(bf16[1536]{0:T(1024)(128)(2,1)S(1)} %dynamic-update-slice, bf16[128]{0:T(256)(128)(2,1)S(1)} %dynamic-update-slice.1, ...), channel_id=2, replica_groups=mesh['dp'=16,'tensor'=2] {'dp'}, use_global_device_ids=true, to_apply=%add | all-reduce | flops 3328 | bytes 13312
  52.2 17.4 all-gather.6
  71.5 21.4 %all-gather.1 = bf16[1,1536,128]{2,1,0:T(8,128)(2,1)S(1)} all-gather(bf16[1,96,128]{2,1,0:T(8,128)(2,1)} %param.22), channel_id=3, replica_groups=mesh['dp'=16,'tensor'=2] {'dp'}, dimensions={1}, use_global_device_ids=true | all-gather | bytes 417792 | tf_op jit(solution)/shard_map/all_gather | solution.py:230
  94.8 12.0 all_gather.54
  107.9 18.2 all-gather.3
  128.8 2.4 fusion.27
  136.8 3.5 convolution_convert_fusion
  144.4 19.6 %all_gather.66 = bf16[256,1536]{1,0:T(8,128)(2,1)} all-gather(bf16[128,1536]{1,0:T(8,128)(2,1)S(1)} %convert_element_type.173), channel_id=1, replica_groups=mesh['dp'=16,'tensor'=2] {'tensor'}, dimensions={0}, use_global_device_ids=true | all-gather | bytes 1179648 | tf_op jit(solution)/shard_map/all_gather | solution.py:258
  168.4 13.0 collective-permute-done.1
  183.0 31.9 %collective-permute-done.2 = bf16[96,4480]{1,0:T(8,128)(2,1)S(1)} collective-permute-done((bf16[96,4480]{1,0:T(8,128)(2,1)S(1)}, bf16[96,4480]{1,0:T(8,128)(2,1)S(1)}, u32[]{:S(2)}, u32[]{:S(2)}) %collective-permute-start.2) | collective-permute-done | bytes 860192 | tf_op jit(solution)/shard_map/ppermute | solution.py:245
  215.9 21.9 %collective-permute-done.3 = bf16[96,4480]{1,0:T(8,128)(2,1)S(1)} collective-permute-done((bf16[96,4480]{1,0:T(8,128)(2,1)S(1)}, bf16[96,4480]{1,0:T(8,128)(2,1)S(1)}, u32[]{:S(2)}, u32[]{:S(2)}) %collective-permute-start.3) | collective-permute-done | bytes 860192 | tf_op jit(solution)/shard_map/ppermute | solution.py:245
  238.7 32.5 %collective-permute-done.4 = bf16[96,4480]{1,0:T(8,128)(2,1)S(1)} collective-permute-done((bf16[96,4480]{1,0:T(8,128)(2,1)S(1)}, bf16[96,4480]{1,0:T(8,128)(2,1)S(1)}, u32[]{:S(2)}, u32[]{:S(2)}) %collective-permute-start.4) | collective-permute-done | bytes 860192 | tf_op jit(solution)/shard_map/ppermute | solution.py:245
  272.2 31.7 %collective-permute-done.5 = bf16[96,4480]{1,0:T(8,128)(2,1)} collective-permute-done((bf16[96,4480]{1,0:T(8,128)(2,1)S(1)}, bf16[96,4480]{1,0:T(8,128)(2,1)}, u32[]{:S(2)}, u32[]{:S(2)}) %collective-permute-start.5) | collective-permute-done | bytes 860192 | tf_op jit(solution)/shard_map/ppermute | solution.py:245
  308.4 8.6 all_gather.63
  321.3 31.5 %collective-permute-done.7 = bf16[96,4480]{1,0:T(8,128)(2,1)S(1)} collective-permute-done((bf16[96,4480]{1,0:T(8,128)(2,1)}, bf16[96,4480]{1,0:T(8,128)(2,1)S(1)}, u32[]{:S(2)}, u32[]{:S(2)}) %collective-permute-start.7) | collective-permute-done | bytes 860192 | tf_op jit(solution)/shard_map/ppermute | solution.py:245
  353.9 20.2 %collective-permute-done.8 = bf16[96,4480]{1,0:T(8,128)(2,1)S(1)} collective-permute-done((bf16[96,4480]{1,0:T(8,128)(2,1)S(1)}, bf16[96,4480]{1,0:T(8,128)(2,1)S(1)}, u32[]{:S(2)}, u32[]{:S(2)}) %collective-permute-start.8) | collective-permute-done | bytes 860192 | tf_op jit(solution)/shard_map/ppermute | solution.py:245
  375.0 32.5 %collective-permute-done.9 = bf16[96,4480]{1,0:T(8,128)(2,1)S(1)} collective-permute-done((bf16[96,4480]{1,0:T(8,128)(2,1)S(1)}, bf16[96,4480]{1,0:T(8,128)(2,1)S(1)}, u32[]{:S(2)}, u32[]{:S(2)}) %collective-permute-start.9) | collective-permute-done | bytes 860192 | tf_op jit(solution)/shard_map/ppermute | solution.py:245
  408.5 32.2 %collective-permute-done.10 = bf16[96,4480]{1,0:T(8,128)(2,1)S(1)} collective-permute-done((bf16[96,4480]{1,0:T(8,128)(2,1)S(1)}, bf16[96,4480]{1,0:T(8,128)(2,1)S(1)}, u32[]{:S(2)}, u32[]{:S(2)}) %collective-permute-start.10) | collective-permute-done | bytes 860192 | tf_op jit(solution)/shard_map/ppermute | solution.py:245
  441.7 13.9 collective-permute-done.11
  456.6 13.9 collective-permute-done.12
  471.4 14.0 collective-permute-done.13
  486.8 13.9 collective-permute-done.14
  501.7 12.0 gather_fusion
  513.7 11.1 fusion
  524.7 11.2 fusion.6
  535.9 9.4 multiply_convert_fusion
  545.4 8.5 fusion.4
  553.9 8.3 fusion.11
  563.7 12.0 reduce-scatter.21.cloned.1.call-done
  580.0 11.4 all_gather.67
  605.6 2.5 fusion.16
  610.0 10.3 fusion.8
  621.7 5.9 reduce-scatter.23.cloned.1.call-done
  637.8 3.0 fusion.111
  642.0 3.0 fusion.112
  646.0 12.8 fusion.113
  659.0 12.9 fusion.114
  673.0 12.9 fusion.115
  689.1 34.3 %all-reduce.6 = (f32[6,128]{1,0:T(8,128)S(1)}, f32[1,1,128]{2,1,0:T(1,128)}, f32[1,128]{1,0:T(1,128)S(1)}) all-reduce(f32[6,128]{1,0:T(8,128)} %fusion.70, f32[1,1,128]{2,1,0:T(1,128)} %bitcast.269, f32[1,128]{1,0:T(1,128)} %bitcast.268), channel_id=22, replica_groups=mesh['dp'=16,'tensor'=2] {'dp'}, use_global_device_ids=true, to_apply=%region_18.19.clone | all-reduce | flops 1024 | bytes 8192
  725.3 2.8 fusion.46
  728.1 21.3 %reduce-scatter.39.cloned.1.call-done = f32[48,2]{1,0:T(8,128)} async-done(((f32[1536,2]{1,0:T(8,128)}), f32[48,2]{1,0:T(8,128)}) %reduce-scatter.39.cloned.1.call-update) | async-done | bytes 400
  750.8 58.4 %reduce-scatter.27.cloned.1.call-done = f32[96,128]{1,0:T(8,128)} async-done(((f32[1536,128]{1,0:T(8,128)}), f32[96,128]{1,0:T(8,128)}) %reduce-scatter.27.cloned.1.call-update) | async-done | bytes 49168 | tf_op jit(solution)/shard_map/reduce_scatter | solution.py:331
  809.2 59.9 %reduce-scatter.29.cloned.1.call-done = f32[96,128]{1,0:T(8,128)} async-done(((f32[1536,128]{1,0:T(8,128)}), f32[96,128]{1,0:T(8,128)}) %reduce-scatter.29.cloned.1.call-update) | async-done | bytes 49168 | tf_op jit(solution)/shard_map/reduce_scatter | solution.py:332
  869.1 78.9 %reduce-scatter.25.cloned.1.call-done = f32[96,768]{1,0:T(8,128)} async-done(((f32[1536,768]{1,0:T(8,128)}), f32[96,768]{1,0:T(8,128)}) %reduce-scatter.25.cloned.1.call-update) | async-done | bytes 294928 | tf_op jit(solution)/shard_map/reduce_scatter | solution.py:330
  948.0 79.2 %reduce-scatter.31.cloned.1.call-done = f32[768,96]{0,1:T(8,128)} async-done(((f32[768,1536]{0,1:T(8,128)}), f32[768,96]{0,1:T(8,128)}) %reduce-scatter.31.cloned.1.call-update) | async-done | bytes 294928 | tf_op jit(solution)/shard_map/reduce_scatter | solution.py:333
  1027.2 268.5 %reduce-scatter.33.cloned.1.call-done = f32[96,4480]{1,0:T(8,128)} async-done(((f32[1536,4480]{1,0:T(8,128)}), f32[96,4480]{1,0:T(8,128)}) %reduce-scatter.33.cloned.1.call-update) | async-done | bytes 1720336 | tf_op jit(solution)/shard_map/reduce_scatter | solution.py:302
  1295.8 268.4 %reduce-scatter.35.cloned.1.call-done = f32[96,4480]{1,0:T(8,128)} async-done(((f32[1536,4480]{1,0:T(8,128)}), f32[96,4480]{1,0:T(8,128)}) %reduce-scatter.35.cloned.1.call-update) | async-done | bytes 1720336 | tf_op jit(solution)/shard_map/reduce_scatter | solution.py:303
  1564.2 268.4 %reduce-scatter.37.cloned.1.call-done = f32[4480,96]{0,1:T(8,128)} async-done(((f32[4480,1536]{0,1:T(8,128)}), f32[4480,96]{0,1:T(8,128)}) %reduce-scatter.37.cloned.1.call-update) | async-done | bytes 1720336 | tf_op jit(solution)/shard_map/reduce_scatter | solution.py:304
  (218 shorter events, 91.9 us)
Async XLA Ops:
  7.2 100.7 %copy-start.30 = (bf16[1,96,128]{2,1,0:T(8,128)(2,1)S(1)}, bf16[1,96,128]{2,1,0:T(8,128)(2,1)}, u32[]{:S(2)}) copy-start(bf16[1,96,128]{2,1,0:T(8,128)(2,1)} %param.21) | copy-start | bytes 73732
  7.2 121.5 %copy-start.35 = (s32[1,256]{1,0:T(1,128)S(1)}, s32[1,256]{1,0:T(1,128)}, u32[]{:S(2)}) copy-start(s32[1,256]{1,0:T(1,128)} %param.17) | copy-start | bytes 3076
  7.2 121.6 %all-gather.16.cloned.1.call-start = ((), (), s32[]{:S(2)}) async-start(), calls=%async_computation.23 | async-start | bytes 2506752 | tf_op jit(solution)/shard_map/all_gather | solution.py:228
  7.9 128.8 %all-gather.18.cloned.1.call-start = ((), (), s32[]{:S(2)}) async-start(), calls=%async_computation.24 | async-start | bytes 2506752 | tf_op jit(solution)/shard_map/all_gather | solution.py:231
  8.7 297.3 %reduce-scatter.17.cloned.1.call-start = ((), (), s32[]{:S(2)}) async-start(), calls=%async_computation.12 | async-start | bytes 1179648 | tf_op jit(solution)/shard_map/reduce_scatter | solution.py:261
  70.3 60.9 %copy-start.31 = (f32[1,256]{1,0:T(1,128)}, f32[1,256]{1,0:T(1,128)S(1)}, u32[]{:S(2)}) copy-start(f32[1,256]{1,0:T(1,128)S(1)} %convert_element_type.156) | copy-start | bytes 3076
  70.4 58.4 %copy-start.33 = (f32[64]{0:T(128)}, f32[64]{0:T(128)S(1)}, u32[]{:S(2)}) copy-start(f32[64]{0:T(128)S(1)} %multiply_exponential_fusion) | copy-start | bytes 772
  93.0 13.9 copy-start.9
  126.1 5.5 copy-start.7
  133.3 7.0 copy-start.11
  136.7 29.4 %copy-start.21 = (bf16[128,6,256]{2,0,1:T(8,128)(2,1)}, bf16[128,6,256]{2,0,1:T(8,128)(2,1)S(1)}, u32[]{:S(2)}) copy-start(bf16[128,6,256]{2,0,1:T(8,128)(2,1)S(1)} %convolution_convert_fusion.1) | copy-start | bytes 1179652
  140.3 373.4 %all-gather.22.cloned.1.call-start = ((), (), s32[]{:S(2)}) async-start(), calls=%async_computation.26 | async-start | bytes 14622720 | tf_op jit(solution)/shard_map/all_gather | solution.py:253
  140.9 383.8 %all-gather.20.cloned.1.call-start = ((), (), s32[]{:S(2)}) async-start(), calls=%async_computation.25 | async-start | bytes 14622720 | tf_op jit(solution)/shard_map/all_gather | solution.py:251
  141.5 434.2 %reduce-scatter.21.cloned.1.call-start = ((), (), s32[]{:S(2)}) async-start(), calls=%async_computation.14 | async-start | bytes 1179648 | tf_op jit(solution)/shard_map/reduce_scatter | solution.py:261
  141.5 24.6 %collective-permute-start = (bf16[96,4480]{1,0:T(8,128)(2,1)}, bf16[96,4480]{1,0:T(8,128)(2,1)}, u32[]{:S(2)}, u32[]{:S(2)}) collective-permute-start(bf16[96,4480]{1,0:T(8,128)(2,1)} %bitcast.262), channel_id=1, source_target_pairs={{0,2},{2,4},{4,6},{6,8},{8,10},{10,12},{12,14},{14,16},{16,18},{18... | collective-permute-start | bytes 2580488 | tf_op jit(solution)/shard_map/ppermute | solution.py:245
  166.2 15.3 collective-permute-start.1
  168.4 137.5 %copy-start = (bf16[128,1536]{1,0:T(8,128)(2,1)S(1)}, bf16[128,1536]{1,0:T(8,128)(2,1)}, u32[]{:S(2)}) copy-start(bf16[128,1536]{1,0:T(8,128)(2,1)} %param.15) | copy-start | bytes 1179652
  181.4 33.5 %collective-permute-start.2 = (bf16[96,4480]{1,0:T(8,128)(2,1)S(1)}, bf16[96,4480]{1,0:T(8,128)(2,1)S(1)}, u32[]{:S(2)}, u32[]{:S(2)}) collective-permute-start(bf16[96,4480]{1,0:T(8,128)(2,1)S(1)} %collective-permute-done.1), channel_id=1, source_target_pairs={{0,2},{2,4},{4,6},{6,8},{8,10},{10,12},{12,14},{14,16},{16,18},{18... | collective-permute-start | bytes 2580488 | tf_op jit(solution)/shard_map/ppermute | solution.py:245
  214.9 22.8 %collective-permute-start.3 = (bf16[96,4480]{1,0:T(8,128)(2,1)S(1)}, bf16[96,4480]{1,0:T(8,128)(2,1)S(1)}, u32[]{:S(2)}, u32[]{:S(2)}) collective-permute-start(bf16[96,4480]{1,0:T(8,128)(2,1)S(1)} %collective-permute-done.2), channel_id=1, source_target_pairs={{0,2},{2,4},{4,6},{6,8},{8,10},{10,12},{12,14},{14,16},{16,18},{18... | collective-permute-start | bytes 2580488 | tf_op jit(solution)/shard_map/ppermute | solution.py:245
  237.7 33.5 %collective-permute-start.4 = (bf16[96,4480]{1,0:T(8,128)(2,1)S(1)}, bf16[96,4480]{1,0:T(8,128)(2,1)S(1)}, u32[]{:S(2)}, u32[]{:S(2)}) collective-permute-start(bf16[96,4480]{1,0:T(8,128)(2,1)S(1)} %collective-permute-done.3), channel_id=1, source_target_pairs={{0,2},{2,4},{4,6},{6,8},{8,10},{10,12},{12,14},{14,16},{16,18},{18... | collective-permute-start | bytes 2580488 | tf_op jit(solution)/shard_map/ppermute | solution.py:245
  271.2 32.6 %collective-permute-start.5 = (bf16[96,4480]{1,0:T(8,128)(2,1)S(1)}, bf16[96,4480]{1,0:T(8,128)(2,1)}, u32[]{:S(2)}, u32[]{:S(2)}) collective-permute-start(bf16[96,4480]{1,0:T(8,128)(2,1)S(1)} %collective-permute-done.4), channel_id=1, source_target_pairs={{0,2},{2,4},{4,6},{6,8},{8,10},{10,12},{12,14},{14,16},{16,18},{18... | collective-permute-start | bytes 2580488 | tf_op jit(solution)/shard_map/ppermute | solution.py:245
  303.8 15.4 collective-permute-start.6
  307.2 9.7 copy-start.32
  319.2 33.7 %collective-permute-start.7 = (bf16[96,4480]{1,0:T(8,128)(2,1)}, bf16[96,4480]{1,0:T(8,128)(2,1)S(1)}, u32[]{:S(2)}, u32[]{:S(2)}) collective-permute-start(bf16[96,4480]{1,0:T(8,128)(2,1)} %collective-permute-done.6), channel_id=1, source_target_pairs={{0,2},{2,4},{4,6},{6,8},{8,10},{10,12},{12,14},{14,16},{16,18},{18... | collective-permute-start | bytes 2580488 | tf_op jit(solution)/shard_map/ppermute | solution.py:245
  352.9 21.2 %collective-permute-start.8 = (bf16[96,4480]{1,0:T(8,128)(2,1)S(1)}, bf16[96,4480]{1,0:T(8,128)(2,1)S(1)}, u32[]{:S(2)}, u32[]{:S(2)}) collective-permute-start(bf16[96,4480]{1,0:T(8,128)(2,1)S(1)} %collective-permute-done.7), channel_id=1, source_target_pairs={{0,2},{2,4},{4,6},{6,8},{8,10},{10,12},{12,14},{14,16},{16,18},{18... | collective-permute-start | bytes 2580488 | tf_op jit(solution)/shard_map/ppermute | solution.py:245
  374.1 33.5 %collective-permute-start.9 = (bf16[96,4480]{1,0:T(8,128)(2,1)S(1)}, bf16[96,4480]{1,0:T(8,128)(2,1)S(1)}, u32[]{:S(2)}, u32[]{:S(2)}) collective-permute-start(bf16[96,4480]{1,0:T(8,128)(2,1)S(1)} %collective-permute-done.8), channel_id=1, source_target_pairs={{0,2},{2,4},{4,6},{6,8},{8,10},{10,12},{12,14},{14,16},{16,18},{18... | collective-permute-start | bytes 2580488 | tf_op jit(solution)/shard_map/ppermute | solution.py:245
  407.5 33.2 %collective-permute-start.10 = (bf16[96,4480]{1,0:T(8,128)(2,1)S(1)}, bf16[96,4480]{1,0:T(8,128)(2,1)S(1)}, u32[]{:S(2)}, u32[]{:S(2)}) collective-permute-start(bf16[96,4480]{1,0:T(8,128)(2,1)S(1)} %collective-permute-done.9), channel_id=1, source_target_pairs={{0,2},{2,4},{4,6},{6,8},{8,10},{10,12},{12,14},{14,16},{16,18},{18... | collective-permute-start | bytes 2580488 | tf_op jit(solution)/shard_map/ppermute | solution.py:245
  440.7 14.9 collective-permute-start.11
  455.6 14.9 collective-permute-start.12
  470.5 14.9 collective-permute-start.13
  485.4 15.3 collective-permute-start.14
  524.7 11.2 copy-start.1
  524.7 11.2 copy-start.4
  545.3 8.5 copy-start.19
  553.9 21.8 %copy-start.2 = (bf16[128,1536]{1,0:T(8,128)(2,1)S(1)}, bf16[128,1536]{1,0:T(8,128)(2,1)}, u32[]{:S(2)}) copy-start(bf16[128,1536]{1,0:T(8,128)(2,1)} %reduce-scatter.17.cloned.1.call-done) | copy-start | bytes 1179652
  562.2 65.4 %reduce-scatter.23.cloned.1.call-start = ((), (), s32[]{:S(2)}) async-start(), calls=%async_computation.15 | async-start | bytes 1179648 | tf_op jit(solution)/shard_map/reduce_scatter | solution.py:261
  575.7 16.6 copy-start.37
  609.9 115.4 %reduce-scatter.19.cloned.1.call-start = ((), (), s32[]{:S(2)}) async-start(), calls=%async_computation.13 | async-start | bytes 1179648 | tf_op jit(solution)/shard_map/reduce_scatter | solution.py:261
  620.3 129.1 %reduce-scatter.39.cloned.1.call-start = ((), (), s32[]{:S(2)}) async-start(), calls=%async_computation.27 | async-start | bytes 811008
  633.1 176.1 %reduce-scatter.27.cloned.1.call-start = ((), (), s32[]{:S(2)}) async-start(), calls=%async_computation.17 | async-start | bytes 835584 | tf_op jit(solution)/shard_map/reduce_scatter | solution.py:331
  635.4 233.7 %reduce-scatter.29.cloned.1.call-start = ((), (), s32[]{:S(2)}) async-start(), calls=%async_computation.18 | async-start | bytes 835584 | tf_op jit(solution)/shard_map/reduce_scatter | solution.py:332
  637.7 310.3 %reduce-scatter.25.cloned.1.call-start = ((), (), s32[]{:S(2)}) async-start(), calls=%async_computation.16 | async-start | bytes 5013504 | tf_op jit(solution)/shard_map/reduce_scatter | solution.py:330
  640.8 386.5 %reduce-scatter.31.cloned.1.call-start = ((), (), s32[]{:S(2)}) async-start(), calls=%async_computation.19 | async-start | bytes 5013504 | tf_op jit(solution)/shard_map/reduce_scatter | solution.py:333
  644.9 650.8 %reduce-scatter.33.cloned.1.call-start = ((), (), s32[]{:S(2)}) async-start(), calls=%async_computation.20 | async-start | bytes 29245440 | tf_op jit(solution)/shard_map/reduce_scatter | solution.py:302
  658.9 905.3 %reduce-scatter.35.cloned.1.call-start = ((), (), s32[]{:S(2)}) async-start(), calls=%async_computation.21 | async-start | bytes 29245440 | tf_op jit(solution)/shard_map/reduce_scatter | solution.py:303
  671.9 1160.7 %reduce-scatter.37.cloned.1.call-start = ((), (), s32[]{:S(2)}) async-start(), calls=%async_computation.22 | async-start | bytes 29245440 | tf_op jit(solution)/shard_map/reduce_scatter | solution.py:304
  685.9 39.3 %copy-start.3 = (f32[128,1536]{1,0:T(8,128)S(1)}, f32[128,1536]{1,0:T(8,128)}, u32[]{:S(2)}) copy-start(f32[128,1536]{1,0:T(8,128)} %param.16) | copy-start | bytes 2359300
  685.9 39.3 %copy-start.15 = (bf16[128,1536]{1,0:T(8,128)(2,1)S(1)}, bf16[128,1536]{1,0:T(8,128)(2,1)}, u32[]{:S(2)}) copy-start(bf16[128,1536]{1,0:T(8,128)(2,1)} %reduce-scatter.21.cloned.1.call-done) | copy-start | bytes 1179652
  (21 other events, 53.4 us)
Sparse Core Ops, SparseCore 0:
  10.3 45.4 all-gather.15
  58.1 41.3 all-gather.17
  140.4 23.6 reduce-scatter.16
  166.3 129.8 all-gather.21
  298.4 138.9 all-gather.19
  562.3 13.3 reduce-scatter.20
  610.0 17.4 reduce-scatter.22
  630.4 17.4 reduce-scatter.18
  653.0 96.3 reduce-scatter.38
  753.4 55.7 reduce-scatter.26
  813.4 55.7 reduce-scatter.28
  873.4 74.5 reduce-scatter.24
  952.4 74.7 reduce-scatter.30
  1031.8 263.9 reduce-scatter.32
  1300.3 263.8 reduce-scatter.34
  1568.7 263.8 reduce-scatter.36
